TPU v7x, 256 devices: a whole 4x4x8 slice. The times are simulated.
256 devices in a mesh: dp: 16 (over z, x_lo), tensor: 16 (over y, x_hi, core).
Axes of the slice: x: 4 (x_hi: 2, x_lo: 2; x = x_hi * 2 + x_lo), y: 4, z: 8, core: 2. Of those that a mesh axis runs over, the one named last changes fastest.
Arguments:
- activations: bfloat16 [8192, 32768], P('tensor', 'dp'), may hold values from -6 to 6
- cotangent: bfloat16 [8192, 32768], P('tensor', 'dp'), may hold values from -6 to 6
- first_up: bfloat16 [64, 128, 128], P('tensor', 'dp'), may hold values from -0.5 to 0.5
- second_up: bfloat16 [128, 64, 256], P('tensor', 'dp'), may hold values from -0.75 to 0.75
- second_down: bfloat16 [128, 64, 256], P('tensor', 'dp'), may hold values from -0.375 to 0.375
- first_down: bfloat16 [64, 128, 128], P('tensor', 'dp'), may hold values from -0.5 to 0.5
Outputs:
- output: bfloat16 [8192, 32768], P('tensor', 'dp')
- grad_input: bfloat16 [8192, 32768], P('tensor', 'dp')
- grad_first_up: float32 [64, 128, 128], P('tensor', 'dp')
- grad_second_up: float32 [128, 64, 256], P('tensor', 'dp')
- grad_second_down: float32 [128, 64, 256], P('tensor', 'dp')
- grad_first_down: float32 [64, 128, 128], P('tensor', 'dp')
All inputs are finite; a program needn't handle non-finite values.
Results may differ from a plain program's by a relative error of at most 0.007.
Values may be sent and summed in bfloat16 or wider, within the bound.
A program may use at most 128 MiB of HBM per device.

v0:
```python
import jax
import jax.numpy as jnp
from jax import lax
from jax.sharding import PartitionSpec as P


def gelu_value(v):
    return 0.5 * v * (1.0 + lax.erf(v * 0.7071067811865476))


def gelu_slope(v):
    return (
        0.5 * (1.0 + lax.erf(v * 0.7071067811865476))
        + v * jnp.exp(-0.5 * v * v) * 0.3989422804014327
    )


def product(form, left, right):
    return jnp.einsum(form, left, right, preferred_element_type=jnp.float32)


def transpose_blocks(values):
    return lax.all_to_all(values, "tensor", split_axis=1, concat_axis=0, tiled=True)


def restore_blocks(values):
    return lax.all_to_all(values, "tensor", split_axis=0, concat_axis=1, tiled=True)


def local(activations, cotangent, first_up, second_up, second_down, first_down):
    width_local, tokens = activations.shape
    blocks_local = first_up.shape[0]
    block_size = first_up.shape[2]
    inputs = activations.reshape(blocks_local, block_size, tokens)
    grads_in = cotangent.reshape(blocks_local, block_size, tokens)
    up_one, up_two, down_two, down_one = (
        lax.all_gather(first_up, "dp", axis=1, tiled=True),
        lax.all_gather(second_up, "dp", axis=1, tiled=True),
        lax.all_gather(second_down, "dp", axis=1, tiled=True),
        lax.all_gather(first_down, "dp", axis=1, tiled=True),
    )
    section_one = product("kit,kij->kjt", inputs, up_one).astype(jnp.bfloat16)
    moved_one = transpose_blocks(section_one)
    pre = product("kjt,jkm->jmt", moved_one, up_two)
    hid = gelu_value(pre).astype(jnp.bfloat16)
    section_three = product("jmt,jkm->kjt", hid, down_two).astype(jnp.bfloat16)
    moved_three = restore_blocks(section_three)
    result = product("kjt,kji->kit", moved_three, down_one).astype(jnp.bfloat16)
    part_r2 = product("kjt,kit->kji", moved_three, grads_in)
    back_three = product("kit,kji->kjt", grads_in, down_one).astype(jnp.bfloat16)
    moved_back = transpose_blocks(back_three)
    part_l2 = product("jmt,kjt->jkm", hid, moved_back)
    back_hid = product("kjt,jkm->jmt", moved_back, down_two)
    back_pre = (back_hid * gelu_slope(pre)).astype(jnp.bfloat16)
    part_l1 = product("kjt,jmt->jkm", moved_one, back_pre)
    back_one = product("jmt,jkm->kjt", back_pre, up_two).astype(jnp.bfloat16)
    local_back = restore_blocks(back_one)
    part_r1 = product("kit,kjt->kij", inputs, local_back)
    grad_in = product("kjt,kij->kit", local_back, up_one).astype(jnp.bfloat16)
    sum_r1, sum_l1, sum_l2, sum_r2 = (
        lax.psum_scatter(part_r1, "dp", scatter_dimension=1, tiled=True),
        lax.psum_scatter(part_l1, "dp", scatter_dimension=1, tiled=True),
        lax.psum_scatter(part_l2, "dp", scatter_dimension=1, tiled=True),
        lax.psum_scatter(part_r2, "dp", scatter_dimension=1, tiled=True),
    )
    output = result.reshape(width_local, tokens)
    grad_input = grad_in.reshape(width_local, tokens)
    return (output, grad_input, sum_r1, sum_l1, sum_l2, sum_r2)


def solution(mesh):
    in_specs = (
        P("tensor", "dp"),
        P("tensor", "dp"),
        P("tensor", "dp", None),
        P("tensor", "dp", None),
        P("tensor", "dp", None),
        P("tensor", "dp", None),
    )
    out_specs = (
        P("tensor", "dp"),
        P("tensor", "dp"),
        P("tensor", "dp", None),
        P("tensor", "dp", None),
        P("tensor", "dp", None),
        P("tensor", "dp", None),
    )
    return jax.shard_map(local, mesh=mesh, in_specs=in_specs, out_specs=out_specs, check_vma=False)
```

profile of v0, /device:TPU:8, one launch (start us, length us, event | category | flops | bytes accessed | tf_op | source)
XLA Modules:
  0.0 613.0 jit_solution(7144741162166313327)
XLA Ops:
  7.2 37.4 %all_gather.12 = bf16[4,128,128]{2,1,0:T(8,128)(2,1)S(1)} all-gather(bf16[4,8,128]{2,1,0:T(8,128)(2,1)} %param.8), channel_id=1, replica_groups=mesh['dp'=16,'tensor'=16] {'dp'}, dimensions={1}, use_global_device_ids=true | all-gather | bytes 139264 | tf_op jit(solution)/shard_map/all_gather | solution.py:37
  48.3 7.2 %all-to-all-start = ((bf16[4,128,2048]{2,0,1:T(4,128)(2,1)}), bf16[4,128,2048]{2,0,1:T(4,128)(2,1)}, u32[]{:S(2)}, u32[]{:S(2)}) async-start(bf16[4,128,2048]{2,0,1:T(4,128)(2,1)} %copy.21), calls=%async_computation | async-start | bytes 4194304 | tf_op jit(solution)/shard_map/all_to_all | solution.py:23
  55.5 50.0 %all_gather.15 = bf16[4,128,128]{2,1,0:T(8,128)(2,1)S(1)} all-gather(bf16[4,8,128]{2,1,0:T(8,128)(2,1)S(1)} %copy-done.5), channel_id=1, replica_groups=mesh['dp'=16,'tensor'=16] {'dp'}, dimensions={1}, use_global_device_ids=true | all-gather | bytes 139264 | tf_op jit(solution)/shard_map/all_gather | solution.py:40
  110.8 7.2 %all-to-all-start.2 = ((bf16[4,128,2048]{2,0,1:T(4,128)(2,1)}), bf16[4,128,2048]{2,0,1:T(4,128)(2,1)}, u32[]{:S(2)}, u32[]{:S(2)}) async-start(bf16[4,128,2048]{2,0,1:T(4,128)(2,1)} %copy.30), calls=%async_computation.2 | async-start | bytes 4194304 | tf_op jit(solution)/shard_map/all_to_all | solution.py:23
  118.0 51.3 %all_gather.13 = bf16[8,64,256]{2,0,1:T(8,128)(2,1)S(1)} all-gather(bf16[8,4,256]{2,0,1:T(8,128)(2,1)S(1)} %copy.23), channel_id=1, replica_groups=mesh['dp'=16,'tensor'=16] {'dp'}, dimensions={1}, use_global_device_ids=true | all-gather | bytes 278528 | tf_op jit(solution)/shard_map/all_gather | solution.py:38
  169.3 31.1 %all_gather.14 = bf16[8,64,256]{2,0,1:T(8,128)(2,1)S(1)} all-gather(bf16[8,4,256]{2,0,1:T(8,128)(2,1)S(1)} %copy.25), channel_id=1, replica_groups=mesh['dp'=16,'tensor'=16] {'dp'}, dimensions={1}, use_global_device_ids=true | all-gather | bytes 278528 | tf_op jit(solution)/shard_map/all_gather | solution.py:39
  200.4 4.3 copy.80
  204.7 3.9 all_to_all.55
  208.6 4.3 copy.79
  212.9 4.0 all_to_all.63
  216.9 7.5 %fusion.7 = (bf16[8,256,2048]{1,2,0:T(8,128)(2,1)}, f32[8,2048,256]{2,1,0:T(8,128)S(1)}) fusion(bf16[64,8,2048]{2,0,1:T(8,128)(2,1)} %all_to_all.55, bf16[8,64,256]{2,0,1:T(8,128)(2,1)S(1)} %all_gather.13), kind=kOutput, calls=%fused_computation.10 | convolution fusion | flops 557842432 | bytes 27525120 | tf_op jit(solution)/shard_map/kjt,jkm->jmt/dot_general | solution.py:19
  224.4 8.5 %fusion.5 = bf16[8,256,2048]{1,2,0:T(8,128)(2,1)S(1)} fusion(f32[8,2048,256]{2,1,0:T(8,128)S(1)} %get-tuple-element.19, bf16[64,8,2048]{2,0,1:T(8,128)(2,1)S(1)} %copy-done.2, bf16[8,64,256]{2,0,1:T(8,128)(2,1)S(1)} %all_gather.14), kind=kOutput, calls=%fused_computation.6 | convolution fusion | flops 578813952 | bytes 27525120 | tf_op jit(solution)/shard_map/kjt,jkm->jmt/dot_general | solution.py:19
  238.6 7.3 %all-to-all-start.3 = ((bf16[64,8,2048]{2,1,0:T(8,128)(2,1)}), bf16[64,8,2048]{2,1,0:T(8,128)(2,1)}, u32[]{:S(2)}, u32[]{:S(2)}) async-start(bf16[64,8,2048]{2,1,0:T(8,128)(2,1)} %copy.35), calls=%async_computation.3 | async-start | bytes 4194304 | tf_op jit(solution)/shard_map/all_to_all | solution.py:27
  245.9 5.5 fusion.30
  252.5 6.0 fusion.10
  261.0 13.4 %all-to-all-done.3 = bf16[64,8,2048]{2,1,0:T(8,128)(2,1)} async-done(((bf16[64,8,2048]{2,1,0:T(8,128)(2,1)}), bf16[64,8,2048]{2,1,0:T(8,128)(2,1)}, u32[]{:S(2)}, u32[]{:S(2)}) %all-to-all-start.3) | async-done | bytes 2097184 | tf_op jit(solution)/shard_map/all_to_all | solution.py:27
  274.4 6.5 %all-to-all-start.1 = ((bf16[64,8,2048]{2,1,0:T(8,128)(2,1)}), bf16[64,8,2048]{2,1,0:T(8,128)(2,1)}, u32[]{:S(2)}, u32[]{:S(2)}) async-start(bf16[64,8,2048]{2,1,0:T(8,128)(2,1)} %copy.28), calls=%async_computation.1 | async-start | bytes 4194304 | tf_op jit(solution)/shard_map/all_to_all | solution.py:27
  281.2 5.5 fusion.31
  289.1 34.2 %reduce-scatter.4.cloned.1.call-done = f32[8,4,256]{2,0,1:T(8,128)} async-done(((f32[8,64,256]{2,0,1:T(8,128)}), f32[8,4,256]{2,0,1:T(8,128)}) %reduce-scatter.4.cloned.1.call-update) | async-done | bytes 32784 | tf_op jit(solution)/shard_map/reduce_scatter | solution.py:62
  324.7 70.0 %reduce-scatter.6.cloned.1.call-done = f32[8,4,256]{2,0,1:T(8,128)} async-done(((f32[8,64,256]{2,0,1:T(8,128)}), f32[8,4,256]{2,0,1:T(8,128)}) %reduce-scatter.6.cloned.1.call-update) | async-done | bytes 32784 | tf_op jit(solution)/shard_map/reduce_scatter | solution.py:63
  399.3 3.6 fusion.12
  406.6 3.7 convolution_convert_fusion.4
  410.2 123.3 %all-reduce.3.cloned.1.call-done = f32[4,128,128]{2,0,1:T(4,128)} async-done(((f32[4,128,128]{2,0,1:T(4,128)}), f32[4,128,128]{2,0,1:T(4,128)}) %all-reduce.3.cloned.1.call-update) | async-done | bytes 262160
  534.8 71.7 %reduce-scatter.8.cloned.1.call-done = f32[4,8,128]{2,1,0:T(8,128)} async-done(((f32[4,128,128]{2,1,0:T(8,128)}), f32[4,8,128]{2,1,0:T(8,128)}) %reduce-scatter.8.cloned.1.call-update) | async-done | bytes 16400 | tf_op jit(solution)/shard_map/reduce_scatter | solution.py:64
  (44 shorter events, 31.3 us)
Async XLA Ops:
  7.2 37.4 %copy-start = (bf16[512,2048]{1,0:T(8,128)(2,1)S(1)}, bf16[512,2048]{1,0:T(8,128)(2,1)}, u32[]{:S(2)}) copy-start(bf16[512,2048]{1,0:T(8,128)(2,1)} %param.6) | copy-start | bytes 6291460
  48.3 7.2 %copy-start.5 = (bf16[4,8,128]{2,1,0:T(8,128)(2,1)S(1)}, bf16[4,8,128]{2,1,0:T(8,128)(2,1)}, u32[]{:S(2)}) copy-start(bf16[4,8,128]{2,1,0:T(8,128)(2,1)} %param.11) | copy-start | bytes 24580
  48.3 62.5 %all-to-all-start = ((bf16[4,128,2048]{2,0,1:T(4,128)(2,1)}), bf16[4,128,2048]{2,0,1:T(4,128)(2,1)}, u32[]{:S(2)}, u32[]{:S(2)}) async-start(bf16[4,128,2048]{2,0,1:T(4,128)(2,1)} %copy.21), calls=%async_computation | async-start | bytes 4194304 | tf_op jit(solution)/shard_map/all_to_all | solution.py:23
  110.8 7.2 %copy-start.3 = (bf16[8,4,256]{2,1,0:T(4,128)(2,1)S(1)}, bf16[8,4,256]{2,1,0:T(4,128)(2,1)}, u32[]{:S(2)}) copy-start(bf16[8,4,256]{2,1,0:T(4,128)(2,1)} %param.9) | copy-start | bytes 49156
  110.8 7.2 %copy-start.4 = (bf16[8,4,256]{2,1,0:T(4,128)(2,1)S(1)}, bf16[8,4,256]{2,1,0:T(4,128)(2,1)}, u32[]{:S(2)}) copy-start(bf16[8,4,256]{2,1,0:T(4,128)(2,1)} %param.10) | copy-start | bytes 49156
  110.8 97.8 %all-to-all-start.2 = ((bf16[4,128,2048]{2,0,1:T(4,128)(2,1)}), bf16[4,128,2048]{2,0,1:T(4,128)(2,1)}, u32[]{:S(2)}, u32[]{:S(2)}) async-start(bf16[4,128,2048]{2,0,1:T(4,128)(2,1)} %copy.30), calls=%async_computation.2 | async-start | bytes 4194304 | tf_op jit(solution)/shard_map/all_to_all | solution.py:23
  216.9 7.5 %copy-start.2 = (bf16[64,8,2048]{2,0,1:T(8,128)(2,1)S(1)}, bf16[64,8,2048]{2,0,1:T(8,128)(2,1)}, u32[]{:S(2)}) copy-start(bf16[64,8,2048]{2,0,1:T(8,128)(2,1)} %all_to_all.63) | copy-start | bytes 6291460
  232.8 3.2 copy-start.1
  238.6 35.8 %all-to-all-start.3 = ((bf16[64,8,2048]{2,1,0:T(8,128)(2,1)}), bf16[64,8,2048]{2,1,0:T(8,128)(2,1)}, u32[]{:S(2)}, u32[]{:S(2)}) async-start(bf16[64,8,2048]{2,1,0:T(8,128)(2,1)} %copy.35), calls=%async_computation.3 | async-start | bytes 4194304 | tf_op jit(solution)/shard_map/all_to_all | solution.py:27
  245.9 77.5 %reduce-scatter.4.cloned.1.call-start = ((), (), s32[]{:S(2)}) async-start(), calls=%async_computation.7 | async-start | bytes 557056 | tf_op jit(solution)/shard_map/reduce_scatter | solution.py:62
  274.4 124.9 %all-to-all-start.1 = ((bf16[64,8,2048]{2,1,0:T(8,128)(2,1)}), bf16[64,8,2048]{2,1,0:T(8,128)(2,1)}, u32[]{:S(2)}, u32[]{:S(2)}) async-start(bf16[64,8,2048]{2,1,0:T(8,128)(2,1)} %copy.28), calls=%async_computation.1 | async-start | bytes 4194304 | tf_op jit(solution)/shard_map/all_to_all | solution.py:27
  280.9 6.9 %copy-start.6 = (u32[256]{0:T(256)S(1)}, u32[256]{0:T(256)}, u32[]{:S(2)}) copy-start(u32[256]{0:T(256)} %constant.16) | copy-start | bytes 3076
  280.9 113.8 %reduce-scatter.6.cloned.1.call-start = ((), (), s32[]{:S(2)}) async-start(), calls=%async_computation.8 | async-start | bytes 557056 | tf_op jit(solution)/shard_map/reduce_scatter | solution.py:63
  287.8 245.7 %all-reduce.3.cloned.1.call-start = ((), (), s32[]{:S(2)}) async-start(), calls=%async_computation.10 | async-start | bytes 524288
  399.2 207.3 %reduce-scatter.8.cloned.1.call-start = ((), (), s32[]{:S(2)}) async-start(), calls=%async_computation.9 | async-start | bytes 278528 | tf_op jit(solution)/shard_map/reduce_scatter | solution.py:64
Sparse Core Ops, SparseCore 0:
  252.6 70.6 reduce-scatter.3
  326.0 68.6 reduce-scatter.5
  399.4 134.1 all-reduce.2
  536.6 69.8 reduce-scatter.7
where the time goes:
time: 614 us; the launch traced here: 613 us
  waiting for transfers between devices  313 us (51%)
  blocking collectives  170 us (28%)
  matrix products  51.8 us (8%)
  local copies, waits for them, and re-layouts  35.7 us (6%)
  starting transfers between devices  28.6 us (5%)
  between operations  14.5 us (2%)
    unnamed x5, waiting for transfers between devices  123 us
    reduce_scatter x1, waiting for transfers between devices, local(): lax.psum_scatter(part_r2, 'dp', scatter_dimension=1, tiled=True)  71.7 us
    reduce_scatter x1, waiting for transfers between devices, local(): lax.psum_scatter(part_l2, 'dp', scatter_dimension=1, tiled=True)  70 us
    dot_general x12, matrix products, product(): return jnp.einsum(form, left, right, preferred_element_type=jnp.float32)  51.8 us
    all_gather x1, blocking collectives, local(): lax.all_gather(second_up, 'dp', axis=1, tiled=True)  51.3 us
    all_gather x1, blocking collectives, local(): lax.all_gather(first_down, 'dp', axis=1, tiled=True)  50 us
    all_gather x1, blocking collectives, local(): lax.all_gather(first_up, 'dp', axis=1, tiled=True)  37.4 us
    reduce_scatter x1, waiting for transfers between devices, local(): lax.psum_scatter(part_l1, 'dp', scatter_dimension=1, tiled=True)  34.2 us
  transfers between devices with their start and end apart: 8, of which 5 were waited for; matrix products, arithmetic and copies ran while one was open for 8% of the time, Pallas kernels for 0%

commit v1 on v0

--- a/solution.py
+++ b/solution.py
@@ -2,6 +2,13 @@
 import jax.numpy as jnp
 from jax import lax
 from jax.sharding import PartitionSpec as P
+
+
+def gather_over(x, name, d):
+    n_dev = lax.axis_size(name)
+    shards = jnp.stack([x for _ in range(n_dev)])
+    shards = lax.all_to_all(shards, name, split_axis=0, concat_axis=0)
+    return jnp.concatenate(shards, axis=d)
 
 
 def gelu_value(v):
@@ -36,7 +43,7 @@
     up_one, up_two, down_two, down_one = (
         lax.all_gather(first_up, "dp", axis=1, tiled=True),
         lax.all_gather(second_up, "dp", axis=1, tiled=True),
-        lax.all_gather(second_down, "dp", axis=1, tiled=True),
+        gather_over(second_down, "dp", 1),
         lax.all_gather(first_down, "dp", axis=1, tiled=True),
     )
     section_one = product("kit,kij->kjt", inputs, up_one).astype(jnp.bfloat16)

time: 614 us -> 592 us (0.964)
  blocking collectives: 170 us -> 136 us
  starting transfers between devices: 28.6 us -> 38 us
    all_gather x1 -> x0, blocking collectives: 31.1 us -> none  [local(): lax.all_gather(second_down, 'dp', axis=1, tiled=True)]
    all_to_all x0 -> x1, starting transfers between devices: none -> 9.5 us  [gather_over(): shards = lax.all_to_all(shards, name, split_axis=0, concat_axis=0)]
  transfers between devices with their start and end apart: 8 -> 9, of which waited for: 5 -> 5; matrix products, arithmetic and copies ran while one was open for 8% -> 9% of each run, Pallas kernels for 0% -> 0%
where the time goes in v1:
time: 592 us; the launch traced here: 591 us
  waiting for transfers between devices  314 us (53%)
  blocking collectives  136 us (23%)
  matrix products  51.8 us (9%)
  starting transfers between devices  38 us (6%)
  local copies, waits for them, and re-layouts  37.5 us (6%)
  between operations  14.6 us (2%)
    unnamed x5, waiting for transfers between devices  123 us
    reduce_scatter x1, waiting for transfers between devices, local(): lax.psum_scatter(part_r2, 'dp', scatter_dimension=1, tiled=True)  71.7 us
    reduce_scatter x1, waiting for transfers between devices, local(): lax.psum_scatter(part_l2, 'dp', scatter_dimension=1, tiled=True)  69.8 us
    dot_general x12, matrix products, product(): return jnp.einsum(form, left, right, preferred_element_type=jnp.float32)  51.8 us
    all_gather x1, blocking collectives, local(): lax.all_gather(second_up, 'dp', axis=1, tiled=True)  51 us
    all_gather x1, blocking collectives, local(): lax.all_gather(first_down, 'dp', axis=1, tiled=True)  50 us
    reduce_scatter x1, waiting for transfers between devices, local(): lax.psum_scatter(part_l1, 'dp', scatter_dimension=1, tiled=True)  35.5 us
    all_gather x1, blocking collectives, local(): lax.all_gather(first_up, 'dp', axis=1, tiled=True)  34.6 us
  transfers between devices with their start and end apart: 9, of which 5 were waited for; matrix products, arithmetic and copies ran while one was open for 9% of the time, Pallas kernels for 0%

profile of v1, /device:TPU:8, one launch (start us, length us, event | category | flops | bytes accessed | tf_op | source)
XLA Modules:
  0.0 590.9 jit_solution(4069069784914590738)
XLA Ops:
  8.9 9.5 %all-to-all-start.1 = ((bf16[16,8,4,256]{3,2,1,0:T(4,128)(2,1)}), bf16[16,8,4,256]{3,2,1,0:T(4,128)(2,1)S(1)}, u32[]{:S(2)}, u32[]{:S(2)}) async-start(bf16[16,8,4,256]{3,2,1,0:T(4,128)(2,1)} %stack.2), calls=%async_computation.1 | async-start | bytes 524288 | tf_op jit(solution)/shard_map/all_to_all | solution.py:10
  18.4 34.6 %all_gather.9 = bf16[4,128,128]{2,1,0:T(8,128)(2,1)S(1)} all-gather(bf16[4,8,128]{2,1,0:T(8,128)(2,1)} %param.8), channel_id=1, replica_groups=mesh['dp'=16,'tensor'=16] {'dp'}, dimensions={1}, use_global_device_ids=true | all-gather | bytes 139264 | tf_op jit(solution)/shard_map/all_gather | solution.py:44
  56.6 7.2 %all-to-all-start = ((bf16[4,128,2048]{2,0,1:T(4,128)(2,1)}), bf16[4,128,2048]{2,0,1:T(4,128)(2,1)}, u32[]{:S(2)}, u32[]{:S(2)}) async-start(bf16[4,128,2048]{2,0,1:T(4,128)(2,1)} %copy.21), calls=%async_computation | async-start | bytes 4194304 | tf_op jit(solution)/shard_map/all_to_all | solution.py:30
  63.9 50.0 %all_gather.11 = bf16[4,128,128]{2,1,0:T(8,128)(2,1)S(1)} all-gather(bf16[4,8,128]{2,1,0:T(8,128)(2,1)S(1)} %copy-done.4), channel_id=1, replica_groups=mesh['dp'=16,'tensor'=16] {'dp'}, dimensions={1}, use_global_device_ids=true | all-gather | bytes 139264 | tf_op jit(solution)/shard_map/all_gather | solution.py:47
  119.2 7.2 %all-to-all-start.3 = ((bf16[4,128,2048]{2,0,1:T(4,128)(2,1)}), bf16[4,128,2048]{2,0,1:T(4,128)(2,1)}, u32[]{:S(2)}, u32[]{:S(2)}) async-start(bf16[4,128,2048]{2,0,1:T(4,128)(2,1)} %copy.29), calls=%async_computation.3 | async-start | bytes 4194304 | tf_op jit(solution)/shard_map/all_to_all | solution.py:30
  126.4 51.0 %all_gather.10 = bf16[8,64,256]{2,0,1:T(8,128)(2,1)S(1)} all-gather(bf16[8,4,256]{2,0,1:T(8,128)(2,1)S(1)} %copy.23), channel_id=1, replica_groups=mesh['dp'=16,'tensor'=16] {'dp'}, dimensions={1}, use_global_device_ids=true | all-gather | bytes 278528 | tf_op jit(solution)/shard_map/all_gather | solution.py:45
  177.5 4.3 copy.74
  181.8 3.9 all_to_all.58
  185.7 4.3 copy.73
  190.0 4.0 all_to_all.67
  193.9 7.5 %fusion.7 = (bf16[8,256,2048]{1,2,0:T(8,128)(2,1)}, f32[8,2048,256]{2,1,0:T(8,128)S(1)}) fusion(bf16[64,8,2048]{2,0,1:T(8,128)(2,1)} %all_to_all.58, bf16[8,64,256]{2,0,1:T(8,128)(2,1)S(1)} %all_gather.10), kind=kOutput, calls=%fused_computation.10 | convolution fusion | flops 557842432 | bytes 27525120 | tf_op jit(solution)/shard_map/kjt,jkm->jmt/dot_general | solution.py:26
  201.4 8.5 %fusion.5 = bf16[8,256,2048]{1,2,0:T(8,128)(2,1)S(1)} fusion(f32[8,2048,256]{2,1,0:T(8,128)S(1)} %get-tuple-element.19, bf16[64,8,2048]{2,0,1:T(8,128)(2,1)S(1)} %copy-done.2, bf16[8,64,256]{2,1,0:T(8,128)(2,1)S(1)} %reshape.34), kind=kOutput, calls=%fused_computation.6 | convolution fusion | flops 578813952 | bytes 27525120 | tf_op jit(solution)/shard_map/kjt,jkm->jmt/dot_general | solution.py:26
  215.7 7.2 %all-to-all-start.4 = ((bf16[64,8,2048]{2,1,0:T(8,128)(2,1)}), bf16[64,8,2048]{2,1,0:T(8,128)(2,1)}, u32[]{:S(2)}, u32[]{:S(2)}) async-start(bf16[64,8,2048]{2,1,0:T(8,128)(2,1)} %copy.33), calls=%async_computation.4 | async-start | bytes 4194304 | tf_op jit(solution)/shard_map/all_to_all | solution.py:34
  222.9 5.5 fusion.28
  229.5 6.0 %fusion.10 = bf16[64,8,2048]{2,0,1:T(8,128)(2,1)S(1)} fusion(bf16[8,256,2048]{1,2,0:T(8,128)(2,1)} %get-tuple-element.18, bf16[8,64,256]{2,1,0:T(8,128)(2,1)S(1)} %reshape.34), kind=kOutput, calls=%fused_computation.19 | convolution fusion | flops 537919488 | bytes 10747904 | tf_op jit(solution)/shard_map/jmt,jkm->kjt/dot_general | solution.py:26
  238.0 13.2 %all-to-all-done.4 = bf16[64,8,2048]{2,1,0:T(8,128)(2,1)} async-done(((bf16[64,8,2048]{2,1,0:T(8,128)(2,1)}), bf16[64,8,2048]{2,1,0:T(8,128)(2,1)}, u32[]{:S(2)}, u32[]{:S(2)}) %all-to-all-start.4) | async-done | bytes 2097184 | tf_op jit(solution)/shard_map/all_to_all | solution.py:34
  251.1 6.5 %all-to-all-start.2 = ((bf16[64,8,2048]{2,1,0:T(8,128)(2,1)}), bf16[64,8,2048]{2,1,0:T(8,128)(2,1)}, u32[]{:S(2)}, u32[]{:S(2)}) async-start(bf16[64,8,2048]{2,1,0:T(8,128)(2,1)} %copy.27), calls=%async_computation.2 | async-start | bytes 4194304 | tf_op jit(solution)/shard_map/all_to_all | solution.py:34
  257.9 5.5 fusion.29
  265.8 35.5 %reduce-scatter.4.cloned.1.call-done = f32[8,4,256]{2,0,1:T(8,128)} async-done(((f32[8,64,256]{2,0,1:T(8,128)}), f32[8,4,256]{2,0,1:T(8,128)}) %reduce-scatter.4.cloned.1.call-update) | async-done | bytes 32784 | tf_op jit(solution)/shard_map/reduce_scatter | solution.py:69
  302.7 69.8 %reduce-scatter.6.cloned.1.call-done = f32[8,4,256]{2,0,1:T(8,128)} async-done(((f32[8,64,256]{2,0,1:T(8,128)}), f32[8,4,256]{2,0,1:T(8,128)}) %reduce-scatter.6.cloned.1.call-update) | async-done | bytes 32784 | tf_op jit(solution)/shard_map/reduce_scatter | solution.py:70
  377.2 3.6 fusion.12
  384.4 3.7 convolution_convert_fusion.4
  388.1 123.3 %all-reduce.3.cloned.1.call-done = f32[4,128,128]{2,0,1:T(4,128)} async-done(((f32[4,128,128]{2,0,1:T(4,128)}), f32[4,128,128]{2,0,1:T(4,128)}) %all-reduce.3.cloned.1.call-update) | async-done | bytes 262160
  512.7 71.7 %reduce-scatter.8.cloned.1.call-done = f32[4,8,128]{2,1,0:T(8,128)} async-done(((f32[4,128,128]{2,1,0:T(8,128)}), f32[4,8,128]{2,1,0:T(8,128)}) %reduce-scatter.8.cloned.1.call-update) | async-done | bytes 16400 | tf_op jit(solution)/shard_map/reduce_scatter | solution.py:71
  (45 shorter events, 33.1 us)
Async XLA Ops:
  7.2 45.8 %copy-start = (bf16[512,2048]{1,0:T(8,128)(2,1)S(1)}, bf16[512,2048]{1,0:T(8,128)(2,1)}, u32[]{:S(2)}) copy-start(bf16[512,2048]{1,0:T(8,128)(2,1)} %param.6) | copy-start | bytes 6291460
  8.9 47.8 %all-to-all-start.1 = ((bf16[16,8,4,256]{3,2,1,0:T(4,128)(2,1)}), bf16[16,8,4,256]{3,2,1,0:T(4,128)(2,1)S(1)}, u32[]{:S(2)}, u32[]{:S(2)}) async-start(bf16[16,8,4,256]{3,2,1,0:T(4,128)(2,1)} %stack.2), calls=%async_computation.1 | async-start | bytes 524288 | tf_op jit(solution)/shard_map/all_to_all | solution.py:10
  56.6 7.2 %copy-start.4 = (bf16[4,8,128]{2,1,0:T(8,128)(2,1)S(1)}, bf16[4,8,128]{2,1,0:T(8,128)(2,1)}, u32[]{:S(2)}) copy-start(bf16[4,8,128]{2,1,0:T(8,128)(2,1)} %param.11) | copy-start | bytes 24580
  56.6 62.5 %all-to-all-start = ((bf16[4,128,2048]{2,0,1:T(4,128)(2,1)}), bf16[4,128,2048]{2,0,1:T(4,128)(2,1)}, u32[]{:S(2)}, u32[]{:S(2)}) async-start(bf16[4,128,2048]{2,0,1:T(4,128)(2,1)} %copy.21), calls=%async_computation | async-start | bytes 4194304 | tf_op jit(solution)/shard_map/all_to_all | solution.py:30
  119.2 7.2 %copy-start.3 = (bf16[8,4,256]{2,1,0:T(4,128)(2,1)S(1)}, bf16[8,4,256]{2,1,0:T(4,128)(2,1)}, u32[]{:S(2)}) copy-start(bf16[8,4,256]{2,1,0:T(4,128)(2,1)} %param.9) | copy-start | bytes 49156
  119.2 66.5 %all-to-all-start.3 = ((bf16[4,128,2048]{2,0,1:T(4,128)(2,1)}), bf16[4,128,2048]{2,0,1:T(4,128)(2,1)}, u32[]{:S(2)}, u32[]{:S(2)}) async-start(bf16[4,128,2048]{2,0,1:T(4,128)(2,1)} %copy.29), calls=%async_computation.3 | async-start | bytes 4194304 | tf_op jit(solution)/shard_map/all_to_all | solution.py:30
  193.9 7.5 %copy-start.2 = (bf16[64,8,2048]{2,0,1:T(8,128)(2,1)S(1)}, bf16[64,8,2048]{2,0,1:T(8,128)(2,1)}, u32[]{:S(2)}) copy-start(bf16[64,8,2048]{2,0,1:T(8,128)(2,1)} %all_to_all.67) | copy-start | bytes 6291460
  209.9 3.2 copy-start.1
  215.7 35.4 %all-to-all-start.4 = ((bf16[64,8,2048]{2,1,0:T(8,128)(2,1)}), bf16[64,8,2048]{2,1,0:T(8,128)(2,1)}, u32[]{:S(2)}, u32[]{:S(2)}) async-start(bf16[64,8,2048]{2,1,0:T(8,128)(2,1)} %copy.33), calls=%async_computation.4 | async-start | bytes 4194304 | tf_op jit(solution)/shard_map/all_to_all | solution.py:34
  222.8 78.5 %reduce-scatter.4.cloned.1.call-start = ((), (), s32[]{:S(2)}) async-start(), calls=%async_computation.8 | async-start | bytes 557056 | tf_op jit(solution)/shard_map/reduce_scatter | solution.py:69
  251.1 126.0 %all-to-all-start.2 = ((bf16[64,8,2048]{2,1,0:T(8,128)(2,1)}), bf16[64,8,2048]{2,1,0:T(8,128)(2,1)}, u32[]{:S(2)}, u32[]{:S(2)}) async-start(bf16[64,8,2048]{2,1,0:T(8,128)(2,1)} %copy.27), calls=%async_computation.2 | async-start | bytes 4194304 | tf_op jit(solution)/shard_map/all_to_all | solution.py:34
  257.7 6.9 %copy-start.5 = (u32[256]{0:T(256)S(1)}, u32[256]{0:T(256)}, u32[]{:S(2)}) copy-start(u32[256]{0:T(256)} %constant.16) | copy-start | bytes 3076
  257.7 114.9 %reduce-scatter.6.cloned.1.call-start = ((), (), s32[]{:S(2)}) async-start(), calls=%async_computation.9 | async-start | bytes 557056 | tf_op jit(solution)/shard_map/reduce_scatter | solution.py:70
  264.5 246.9 %all-reduce.3.cloned.1.call-start = ((), (), s32[]{:S(2)}) async-start(), calls=%async_computation.11 | async-start | bytes 524288
  377.1 207.3 %reduce-scatter.8.cloned.1.call-start = ((), (), s32[]{:S(2)}) async-start(), calls=%async_computation.10 | async-start | bytes 278528 | tf_op jit(solution)/shard_map/reduce_scatter | solution.py:71
Sparse Core Ops, SparseCore 0:
  229.6 71.7 reduce-scatter.3
  304.0 68.4 reduce-scatter.5
  377.2 134.1 all-reduce.2
  514.5 69.8 reduce-scatter.7
